TPU v7x, 512 devices: a whole 4x4x16 slice. The times are simulated.
512 devices in a mesh: dp: 8 (over z_hi, y), mp: 64 (over z_lo, x, core).
Axes of the slice: x: 4, y: 4, z: 16 (z_hi: 2, z_lo: 8; z = z_hi * 8 + z_lo), core: 2. Of those that a mesh axis runs over, the one named last changes fastest.
Arguments:
- tokens: bfloat16 [512, 6144], P(('dp', 'mp')), may hold values from -6 to 6
- w_in: bfloat16 [6144, 24576], P('dp', 'mp'), may hold values from -0.078125 to 0.078125
- w_out: bfloat16 [24576, 6144], P('mp', 'dp'), may hold values from -0.0390625 to 0.0390625
- cotangent: bfloat16 [512, 6144], P(('dp', 'mp')), may hold values from -6 to 6
Outputs:
- mixed: bfloat16 [512, 6144], P(('dp', 'mp'))
- grad_tokens: bfloat16 [512, 6144], P(('dp', 'mp'))
- grad_w_in: float32 [6144, 24576], P('dp', 'mp')
- grad_w_out: float32 [24576, 6144], P('mp', 'dp')
All inputs are finite; a program needn't handle non-finite values.
Results may differ from a plain program's by a relative error of at most 0.0054.
Values may be sent and summed in bfloat16 or wider, within the bound.
No kernel may reach another device: no remote copies, remote signals or barrier semaphores. Data moves between devices by JAX's collectives and lax.ppermute only.
A program may use at most 64 MiB of HBM per device.

v0:
```python
import jax
import jax.numpy as jnp
from jax import lax
from jax.sharding import PartitionSpec as P

epsilon = 1e-06


def gelu_tanh(values):
    return jax.nn.gelu(values, approximate=True)


def gelu_grad(pre_values, upstream):
    return jax.vjp(gelu_tanh, pre_values)[1](upstream)[0]


def spread(local_rows):
    row_count, feature_count = local_rows.shape
    groups = lax.axis_size("dp")
    width_block = feature_count // groups
    gathered = lax.all_gather(local_rows, "mp", axis=0, tiled=True)
    shaped = gathered.reshape(1, gathered.shape[0], groups, width_block)
    traded = lax.all_to_all(shaped, "dp", split_axis=2, concat_axis=0, tiled=True)
    return traded.reshape(groups * traded.shape[1], width_block)


def collect(partial_value, row_count):
    groups = lax.axis_size("dp")
    peer_count = lax.axis_size("mp")
    width_block = partial_value.shape[1]
    shaped = partial_value.reshape(groups, peer_count, row_count, width_block)
    summed = jnp.sum(lax.all_to_all(shaped, "mp", split_axis=1, concat_axis=1, tiled=True), axis=1)
    arrived = lax.all_to_all(summed, "dp", split_axis=0, concat_axis=2, tiled=True)
    return arrived.reshape(row_count, groups * width_block)


def group_total(term):
    return lax.psum(term, "dp")


def local(tokens, w_in, w_out, cotangent):
    contract_last = (((1,), (1,)), ((), ()))
    contract_first = (((0,), (0,)), ((), ()))
    tokens_wide = tokens.astype(jnp.float32)
    row_mean = jnp.mean(tokens_wide, axis=1, keepdims=True)
    centered = tokens_wide - row_mean
    inv_scale = lax.rsqrt(jnp.mean(centered * centered, axis=1, keepdims=True) + epsilon)
    unit_rows = centered * inv_scale
    normed = unit_rows.astype(jnp.bfloat16)
    row_count = tokens.shape[0]
    flat_normed = spread(normed)
    flat_grad = spread(cotangent)
    pre_all = group_total(jnp.dot(flat_normed, w_in, preferred_element_type=jnp.float32))
    act_all = gelu_tanh(pre_all).astype(jnp.bfloat16)
    branch_out = collect(jnp.dot(act_all, w_out, preferred_element_type=jnp.float32), row_count)
    mixed = (tokens_wide + branch_out).astype(jnp.bfloat16)
    act_grad = group_total(
        lax.dot_general(flat_grad, w_out, contract_last, preferred_element_type=jnp.float32)
    )
    pre_grad = gelu_grad(pre_all, act_grad).astype(jnp.bfloat16)
    grad_w_out = lax.dot_general(
        act_all, flat_grad, contract_first, preferred_element_type=jnp.float32
    )
    grad_w_in = lax.dot_general(
        flat_normed, pre_grad, contract_first, preferred_element_type=jnp.float32
    )
    normed_grad = collect(
        lax.dot_general(pre_grad, w_in, contract_last, preferred_element_type=jnp.float32),
        row_count,
    )
    row_inner = jnp.mean(normed_grad * unit_rows, axis=1, keepdims=True)
    through = inv_scale * (
        normed_grad - jnp.mean(normed_grad, axis=1, keepdims=True) - unit_rows * row_inner
    )
    grad_tokens = (cotangent.astype(jnp.float32) + through).astype(jnp.bfloat16)
    return (mixed, grad_tokens, grad_w_in, grad_w_out)


def solution(mesh):
    return jax.shard_map(
        local,
        mesh=mesh,
        in_specs=(P(("dp", "mp"), None), P("dp", "mp"), P("mp", "dp"), P(("dp", "mp"), None)),
        out_specs=(P(("dp", "mp"), None), P(("dp", "mp"), None), P("dp", "mp"), P("mp", "dp")),
        check_vma=False,
    )
```

profile of v0, /device:TPU:2, one launch (start us, length us, event | category | flops | bytes accessed | tf_op | source)
XLA Modules:
  0.0 757.5 jit_solution(10573223621665218163)
XLA Ops:
  7.2 0.0 copy-start
  7.2 1.5 convert_reduce_fusion
  9.3 1.4 multiply_reduce_fusion.1
  11.4 0.8 convert_bitcast_fusion
  12.2 123.8 %all-gather = bf16[64,1,6144]{2,1,0:T(2,128)(2,1)S(1)} all-gather(bf16[1,1,6144]{2,1,0:T(2,128)(2,1)S(1)} %convert_bitcast_fusion), channel_id=1, replica_groups=mesh['dp'=8,'mp'=64] {'mp'}, dimensions={0}, use_global_device_ids=true | all-gather | bytes 798720 | tf_op jit(solution)/shard_map/all_gather | solution.py:21
  135.9 4.7 reduce.7
  140.6 0.1 copy.14
  140.8 0.0 copy-start.5
  140.8 1.0 copy.10
  141.8 11.4 %all-to-all-start = ((bf16[1,64,8,768]{3,1,0,2:T(8,128)(2,1)}), bf16[1,64,8,768]{3,1,0,2:T(8,128)(2,1)S(1)}, u32[]{:S(2)}, u32[]{:S(2)}) async-start(bf16[1,64,8,768]{3,1,0,2:T(8,128)(2,1)} %copy.10), calls=%async_computation | async-start | bytes 1572864 | tf_op jit(solution)/shard_map/all_to_all | solution.py:23
  153.2 0.0 copy-done.5
  153.2 140.4 %all-gather.1 = bf16[64,1,6144]{2,1,0:T(2,128)(2,1)S(1)} all-gather(bf16[1,1,6144]{2,1,0:T(2,128)(2,1)S(1)} %bitcast.46), channel_id=1, replica_groups=mesh['dp'=8,'mp'=64] {'mp'}, dimensions={0}, use_global_device_ids=true | all-gather | bytes 798720 | tf_op jit(solution)/shard_map/all_gather | solution.py:21
  293.6 5.6 reduce.8
  299.2 1.3 copy.15
  300.5 1.0 copy.12
  301.5 0.0 copy-start.3
  301.5 0.0 all-to-all-done
  301.5 13.5 %all-to-all-start.3 = ((bf16[1,64,8,768]{3,1,0,2:T(8,128)(2,1)}), bf16[1,64,8,768]{3,1,0,2:T(8,128)(2,1)S(1)}, u32[]{:S(2)}, u32[]{:S(2)}) async-start(bf16[1,64,8,768]{3,1,0,2:T(8,128)(2,1)} %copy.12), calls=%async_computation.3 | async-start | bytes 1572864 | tf_op jit(solution)/shard_map/all_to_all | solution.py:23
  315.0 0.0 all-reduce.3.cloned.1.call-start
  315.0 0.0 copy-done
  315.0 1.5 fusion.10
  316.5 19.4 %all-to-all-done.3 = bf16[1,64,8,768]{3,1,0,2:T(8,128)(2,1)S(1)} async-done(((bf16[1,64,8,768]{3,1,0,2:T(8,128)(2,1)}), bf16[1,64,8,768]{3,1,0,2:T(8,128)(2,1)S(1)}, u32[]{:S(2)}, u32[]{:S(2)}) %all-to-all-start.3) | async-done | bytes 786464 | tf_op jit(solution)/shard_map/all_to_all | solution.py:23
  335.9 0.0 copy-start.2
  335.9 0.0 copy-done.3
  335.9 1.5 fusion.11
  337.4 0.0 all-reduce.3.cloned.1.call-update
  337.4 0.0 copy-done.2
  337.4 195.6 %all-reduce.3.cloned.1.call-done = (f32[512,384]{1,0:T(8,128)}, f32[512,384]{1,0:T(8,128)}) async-done(((f32[512,384]{1,0:T(8,128)}, f32[512,384]{1,0:T(8,128)}), (f32[512,384]{1,0:T(8,128)}, f32[512,384]{1,0:T(8,128)})) %all-reduce.3.cloned.1.call-update) | async-done | bytes 1572880 | tf_op jit(solution)/shard_map/psum | solution.py:38
  533.0 1.9 fusion.6
  534.9 0.6 fusion.12
  535.5 2.1 copy.13
  537.6 14.7 %all-to-all-start.4 = ((f32[8,64,1,768]{3,0,2,1:T(8,128)}), f32[8,64,1,768]{3,0,2,1:T(8,128)S(1)}, u32[]{:S(2)}, u32[]{:S(2)}) async-start(f32[8,64,1,768]{3,0,2,1:T(8,128)} %copy.13), calls=%async_computation.4 | async-start | bytes 3145728 | tf_op jit(solution)/shard_map/all_to_all | solution.py:32
  552.3 2.0 fusion.9
  554.3 2.1 copy.11
  556.3 69.7 %all-to-all-done.4 = f32[8,64,1,768]{3,0,2,1:T(8,128)S(1)} async-done(((f32[8,64,1,768]{3,0,2,1:T(8,128)}), f32[8,64,1,768]{3,0,2,1:T(8,128)S(1)}, u32[]{:S(2)}, u32[]{:S(2)}) %all-to-all-start.4) | async-done | bytes 1572896 | tf_op jit(solution)/shard_map/all_to_all | solution.py:32
  626.0 0.0 copy-start.1
  626.0 1.1 copy-done.1
  627.2 8.0 %all-to-all-start.1 = ((f32[8,64,1,768]{3,0,2,1:T(8,128)}), f32[8,64,1,768]{3,0,2,1:T(8,128)S(1)}, u32[]{:S(2)}, u32[]{:S(2)}) async-start(f32[8,64,1,768]{3,0,2,1:T(8,128)} %copy.11), calls=%async_computation.1 | async-start | bytes 3145728 | tf_op jit(solution)/shard_map/all_to_all | solution.py:32
  635.2 3.0 fusion.8
  638.2 1.5 reduce_sum.62
  639.7 0.6 reduce_sum.63
  640.3 68.6 %all-to-all-done.1 = f32[8,64,1,768]{3,0,2,1:T(8,128)S(1)} async-done(((f32[8,64,1,768]{3,0,2,1:T(8,128)}), f32[8,64,1,768]{3,0,2,1:T(8,128)S(1)}, u32[]{:S(2)}, u32[]{:S(2)}) %all-to-all-start.1) | async-done | bytes 1572896 | tf_op jit(solution)/shard_map/all_to_all | solution.py:32
  708.9 7.9 %all-to-all-start.5 = ((f32[8,1,768]{2,1,0:T(1,128)}), f32[8,1,768]{2,1,0:T(1,128)S(1)}, u32[]{:S(2)}, u32[]{:S(2)}) async-start(f32[8,1,768]{2,1,0:T(1,128)} %reduce_sum.63), calls=%async_computation.5 | async-start | bytes 49152 | tf_op jit(solution)/shard_map/all_to_all | solution.py:33
  716.8 0.0 copy-start.4
  716.8 1.6 fusion.13
  718.4 0.1 reduce_sum.60
  718.6 0.6 reduce_sum.61
  719.2 12.6 %all-to-all-done.5 = f32[8,1,768]{2,1,0:T(1,128)S(1)} async-done(((f32[8,1,768]{2,1,0:T(1,128)}), f32[8,1,768]{2,1,0:T(1,128)S(1)}, u32[]{:S(2)}, u32[]{:S(2)}) %all-to-all-start.5) | async-done | bytes 24608 | tf_op jit(solution)/shard_map/all_to_all | solution.py:33
  731.8 3.3 all-to-all-start.2
  735.1 0.7 reduce_sum.64
  736.4 0.0 copy-done.4
  736.4 0.7 multiply_reduce_fusion
  737.7 12.3 %all-to-all-done.2 = f32[8,1,768]{2,1,0:T(1,128)S(1)} async-done(((f32[8,1,768]{2,1,0:T(1,128)}), f32[8,1,768]{2,1,0:T(1,128)S(1)}, u32[]{:S(2)}, u32[]{:S(2)}) %all-to-all-start.2) | async-done | bytes 24608 | tf_op jit(solution)/shard_map/all_to_all | solution.py:33
  750.0 0.7 add_convert_fusion
Async XLA Ops:
  7.2 307.9 %copy-start = (bf16[768,384]{1,0:T(8,128)(2,1)S(1)}, bf16[768,384]{1,0:T(8,128)(2,1)}, u32[]{:S(2)}) copy-start(bf16[768,384]{1,0:T(8,128)(2,1)} %param.5) | copy-start | bytes 1769476
  140.8 12.4 %copy-start.5 = (bf16[1,6144]{1,0:T(2,128)(2,1)S(1)}, bf16[1,6144]{1,0:T(2,128)(2,1)}, u32[]{:S(2)}) copy-start(bf16[1,6144]{1,0:T(2,128)(2,1)} %param.7) | copy-start | bytes 36868
  141.8 159.7 %all-to-all-start = ((bf16[1,64,8,768]{3,1,0,2:T(8,128)(2,1)}), bf16[1,64,8,768]{3,1,0,2:T(8,128)(2,1)S(1)}, u32[]{:S(2)}, u32[]{:S(2)}) async-start(bf16[1,64,8,768]{3,1,0,2:T(8,128)(2,1)} %copy.10), calls=%async_computation | async-start | bytes 1572864 | tf_op jit(solution)/shard_map/all_to_all | solution.py:23
  301.5 34.4 %copy-start.3 = (bf16[384,768]{1,0:T(8,128)(2,1)S(1)}, bf16[384,768]{1,0:T(8,128)(2,1)}, u32[]{:S(2)}) copy-start(bf16[384,768]{1,0:T(8,128)(2,1)} %param.6) | copy-start | bytes 1769476
  301.5 34.4 %all-to-all-start.3 = ((bf16[1,64,8,768]{3,1,0,2:T(8,128)(2,1)}), bf16[1,64,8,768]{3,1,0,2:T(8,128)(2,1)S(1)}, u32[]{:S(2)}, u32[]{:S(2)}) async-start(bf16[1,64,8,768]{3,1,0,2:T(8,128)(2,1)} %copy.12), calls=%async_computation.3 | async-start | bytes 1572864 | tf_op jit(solution)/shard_map/all_to_all | solution.py:23
  315.0 218.0 %all-reduce.3.cloned.1.call-start = ((), (), s32[]{:S(2)}) async-start(), calls=%async_computation.6 | async-start | bytes 3145728 | tf_op jit(solution)/shard_map/psum | solution.py:38
  335.9 1.5 copy-start.2
  537.6 88.4 %all-to-all-start.4 = ((f32[8,64,1,768]{3,0,2,1:T(8,128)}), f32[8,64,1,768]{3,0,2,1:T(8,128)S(1)}, u32[]{:S(2)}, u32[]{:S(2)}) async-start(f32[8,64,1,768]{3,0,2,1:T(8,128)} %copy.13), calls=%async_computation.4 | async-start | bytes 3145728 | tf_op jit(solution)/shard_map/all_to_all | solution.py:32
  626.0 1.1 copy-start.1
  627.2 81.8 %all-to-all-start.1 = ((f32[8,64,1,768]{3,0,2,1:T(8,128)}), f32[8,64,1,768]{3,0,2,1:T(8,128)S(1)}, u32[]{:S(2)}, u32[]{:S(2)}) async-start(f32[8,64,1,768]{3,0,2,1:T(8,128)} %copy.11), calls=%async_computation.1 | async-start | bytes 3145728 | tf_op jit(solution)/shard_map/all_to_all | solution.py:32
  708.9 22.8 %all-to-all-start.5 = ((f32[8,1,768]{2,1,0:T(1,128)}), f32[8,1,768]{2,1,0:T(1,128)S(1)}, u32[]{:S(2)}, u32[]{:S(2)}) async-start(f32[8,1,768]{2,1,0:T(1,128)} %reduce_sum.63), calls=%async_computation.5 | async-start | bytes 49152 | tf_op jit(solution)/shard_map/all_to_all | solution.py:33
  716.8 19.6 %copy-start.4 = (bf16[1,6144]{1,0:T(2,128)(2,1)S(1)}, bf16[1,6144]{1,0:T(2,128)(2,1)}, u32[]{:S(2)}) copy-start(bf16[1,6144]{1,0:T(2,128)(2,1)} %param.4) | copy-start | bytes 36868
  731.8 18.2 %all-to-all-start.2 = ((f32[8,1,768]{2,1,0:T(1,128)}), f32[8,1,768]{2,1,0:T(1,128)S(1)}, u32[]{:S(2)}, u32[]{:S(2)}) async-start(f32[8,1,768]{2,1,0:T(1,128)} %reduce_sum.61), calls=%async_computation.2 | async-start | bytes 49152 | tf_op jit(solution)/shard_map/all_to_all | solution.py:33
Sparse Core Ops, SparseCore 0:
  337.5 195.4 all-reduce.2
where the time goes:
time: 758 us
  waiting for transfers between devices  378 us (50%)
  blocking collectives  264 us (35%)
  starting transfers between devices  58.8 us (8%)
  other arithmetic  19.5 us (3%)
  between operations  16.8 us (2%)
  matrix products  10.1 us (1%)
  local copies, waits for them, and re-layouts  10 us (1%)
    all_gather x2, blocking collectives, spread(): gathered = lax.all_gather(local_rows, 'mp', axis=0, tiled=True)  264 us
    psum x1, waiting for transfers between devices, group_total(): return lax.psum(term, 'dp')  196 us
    all_to_all x2, waiting for transfers between devices, collect(): lax.all_to_all(shaped, 'mp', split_axis=1, concat_axis=1, tiled=True)  138 us
    all_to_all x2, starting transfers between devices, spread(): lax.all_to_all(shaped, 'dp', split_axis=2, concat_axis=0, tiled=True)  24.9 us
    all_to_all x2, waiting for transfers between devices, collect(): lax.all_to_all(summed, 'dp', split_axis=0, concat_axis=2, tiled=True)  24.9 us
    all_to_all x2, starting transfers between devices, collect(): lax.all_to_all(shaped, 'mp', split_axis=1, concat_axis=1, tiled=True)  22.7 us
    all_to_all x2, waiting for transfers between devices, spread(): lax.all_to_all(shaped, 'dp', split_axis=2, concat_axis=0, tiled=True)  19.4 us
  transfers between devices with their start and end apart: 7, of which 6 were waited for; matrix products, arithmetic and copies ran while one was open for 3% of the time, Pallas kernels for 0%

commit v1 on v0

--- a/solution.py
+++ b/solution.py
@@ -4,6 +4,10 @@
 from jax.sharding import PartitionSpec as P
 
 epsilon = 1e-06
+
+
+def obtain_slots_on(message):
+    return jnp.sum(jax.lax.all_gather(message, "dp"), 0)
 
 
 def gelu_tanh(values):
@@ -35,7 +39,7 @@
 
 
 def group_total(term):
-    return lax.psum(term, "dp")
+    return obtain_slots_on(term)
 
 
 def local(tokens, w_in, w_out, cotangent):

time: 758 us -> 921 us (1.22)
  blocking collectives: 264 us -> 398 us
  waiting for transfers between devices: 378 us -> 413 us
  starting transfers between devices: 58.8 us -> 49 us
    all_gather x0 -> x2, waiting for transfers between devices: none -> 250 us  [obtain_slots_on(): return jnp.sum(jax.lax.all_gather(message, 'dp'), 0)]
    psum x1 -> x0, waiting for transfers between devices: 196 us -> none  [group_total(): return lax.psum(term, 'dp')]
    all_to_all x0 -> x2, blocking collectives: none -> 72.4 us  [spread(): lax.all_to_all(shaped, 'dp', split_axis=2, concat_axis=0, tiled=True)]
    all_gather x2, blocking collectives: 264 us -> 325 us  [spread(): gathered = lax.all_gather(local_rows, 'mp', axis=0, tiled=True)]
    all_to_all x2 -> x0, starting transfers between devices: 24.9 us -> none  [spread(): lax.all_to_all(shaped, 'dp', split_axis=2, concat_axis=0, tiled=True)]
    all_to_all x2 -> x0, waiting for transfers between devices: 19.4 us -> none  [spread(): lax.all_to_all(shaped, 'dp', split_axis=2, concat_axis=0, tiled=True)]
    all_to_all x2, starting transfers between devices: 22.7 us -> 37.2 us  [collect(): lax.all_to_all(shaped, 'mp', split_axis=1, concat_axis=1, tiled=True)]
  transfers between devices with their start and end apart: 7 -> 6, of which waited for: 6 -> 5; matrix products, arithmetic and copies ran while one was open for 3% -> 3% of each run, Pallas kernels for 0% -> 0%
where the time goes in v1:
time: 921 us; the launch traced here: 920 us
  waiting for transfers between devices  413 us (45%)
  blocking collectives  398 us (43%)
  starting transfers between devices  49 us (5%)
  other arithmetic  27.9 us (3%)
  between operations  16.8 us (2%)
    all_gather x2, blocking collectives, spread(): gathered = lax.all_gather(local_rows, 'mp', axis=0, tiled=True)  325 us
    all_gather x2, waiting for transfers between devices, obtain_slots_on(): return jnp.sum(jax.lax.all_gather(message, 'dp'), 0)  250 us
    all_to_all x2, waiting for transfers between devices, collect(): lax.all_to_all(shaped, 'mp', split_axis=1, concat_axis=1, tiled=True)  140 us
    all_to_all x2, blocking collectives, spread(): lax.all_to_all(shaped, 'dp', split_axis=2, concat_axis=0, tiled=True)  72.4 us
    all_to_all x2, starting transfers between devices, collect(): lax.all_to_all(shaped, 'mp', split_axis=1, concat_axis=1, tiled=True)  37.2 us
    all_to_all x2, waiting for transfers between devices, collect(): lax.all_to_all(summed, 'dp', split_axis=0, concat_axis=2, tiled=True)  23.4 us
  transfers between devices with their start and end apart: 6, of which 5 were waited for; matrix products, arithmetic and copies ran while one was open for 3% of the time, Pallas kernels for 0%

profile of v1, /device:TPU:2, one launch (start us, length us, event | category | flops | bytes accessed | tf_op | source)
XLA Modules:
  0.0 920.3 jit_solution(292134303519451277)
XLA Ops:
  7.2 0.0 copy-start
  7.2 0.0 all-gather.7.cloned.1.call-start
  7.2 1.4 convert_reduce_fusion
  9.3 1.4 multiply_reduce_fusion.1
  11.4 0.8 convert_bitcast_fusion
  12.2 122.7 %all-gather.2 = bf16[64,1,6144]{2,1,0:T(2,128)(2,1)S(1)} all-gather(bf16[1,1,6144]{2,1,0:T(2,128)(2,1)S(1)} %convert_bitcast_fusion), channel_id=1, replica_groups=mesh['dp'=8,'mp'=64] {'mp'}, dimensions={0}, use_global_device_ids=true | all-gather | bytes 798720 | tf_op jit(solution)/shard_map/all_gather | solution.py:25
  134.9 4.7 reduce.7
  139.6 0.1 copy.14
  139.7 0.1 copy.10
  139.9 34.1 %all_to_all.58 = bf16[1,64,8,768]{3,1,0,2:T(8,128)(2,1)S(1)} all-to-all(bf16[1,64,8,768]{3,1,0,2:T(8,128)(2,1)S(1)} %copy.10), channel_id=1, replica_groups=mesh['dp'=8,'mp'=64] {'dp'}, dimensions={2} | all-to-all | bytes 1572864 | tf_op jit(solution)/shard_map/all_to_all | solution.py:27
  174.0 0.0 copy-start.3
  174.0 0.0 copy-done
  174.0 1.5 fusion.10
  175.4 0.0 all-gather.7.cloned.1.call-update
  175.4 0.0 all-gather.9.cloned.1.call-start
  175.5 0.0 copy-done.3
  175.5 202.8 %all-gather.3 = bf16[64,1,6144]{2,1,0:T(2,128)(2,1)S(1)} all-gather(bf16[1,1,6144]{2,1,0:T(2,128)(2,1)S(1)} %bitcast.50), channel_id=1, replica_groups=mesh['dp'=8,'mp'=64] {'mp'}, dimensions={0}, use_global_device_ids=true | all-gather | bytes 798720 | tf_op jit(solution)/shard_map/all_gather | solution.py:25
  378.3 5.6 reduce.8
  383.9 1.4 copy.15
  385.3 0.0 copy-start.1
  385.3 0.1 copy.12
  385.4 38.4 %all_to_all.59 = bf16[1,64,8,768]{3,1,0,2:T(8,128)(2,1)S(1)} all-to-all(bf16[1,64,8,768]{3,1,0,2:T(8,128)(2,1)S(1)} %copy.12), channel_id=1, replica_groups=mesh['dp'=8,'mp'=64] {'dp'}, dimensions={2} | all-to-all | bytes 1572864 | tf_op jit(solution)/shard_map/all_to_all | solution.py:27
  423.8 0.0 copy-done.1
  423.8 1.5 fusion.11
  425.3 0.0 all-gather.9.cloned.1.call-update
  425.3 0.0 all-gather.7.cloned.1.call-done
  425.3 3.2 reduce_sum.78
  428.5 249.7 %all-gather.9.cloned.1.call-done = f32[4096,384]{1,0:T(8,128)} async-done(((f32[512,384]{1,0:T(8,128)}), f32[4096,384]{1,0:T(8,128)}) %all-gather.9.cloned.1.call-update) | async-done | bytes 6291472 | tf_op jit(solution)/shard_map/all_gather | solution.py:10
  678.2 4.0 reduce_sum.81
  682.3 1.7 fusion.6
  683.9 0.6 fusion.12
  684.5 2.1 copy.13
  686.6 28.8 %all-to-all-start.4 = ((f32[8,64,1,768]{3,0,2,1:T(8,128)}), f32[8,64,1,768]{3,0,2,1:T(8,128)}, u32[]{:S(2)}, u32[]{:S(2)}) async-start(f32[8,64,1,768]{3,0,2,1:T(8,128)} %copy.13), calls=%async_computation.4 | async-start | bytes 3145728 | tf_op jit(solution)/shard_map/all_to_all | solution.py:36
  715.3 1.7 fusion.9
  717.1 2.1 copy.11
  719.1 69.9 %all-to-all-done.4 = f32[8,64,1,768]{3,0,2,1:T(8,128)} async-done(((f32[8,64,1,768]{3,0,2,1:T(8,128)}), f32[8,64,1,768]{3,0,2,1:T(8,128)}, u32[]{:S(2)}, u32[]{:S(2)}) %all-to-all-start.4) | async-done | bytes 1572896 | tf_op jit(solution)/shard_map/all_to_all | solution.py:36
  789.0 8.4 all-to-all-start.1
  797.4 1.6 fusion.8
  799.0 1.5 reduce_sum.82
  800.6 0.6 reduce_sum.83
  801.2 69.9 %all-to-all-done.1 = f32[8,64,1,768]{3,0,2,1:T(8,128)} async-done(((f32[8,64,1,768]{3,0,2,1:T(8,128)}), f32[8,64,1,768]{3,0,2,1:T(8,128)}, u32[]{:S(2)}, u32[]{:S(2)}) %all-to-all-start.1) | async-done | bytes 1572896 | tf_op jit(solution)/shard_map/all_to_all | solution.py:36
  871.1 8.5 all-to-all-start.5
  879.6 0.0 copy-start.2
  879.6 1.6 fusion.13
  881.2 1.5 reduce_sum.79
  882.7 0.6 reduce_sum.80
  883.3 11.2 %all-to-all-done.5 = f32[8,1,768]{2,1,0:T(1,128)S(1)} async-done(((f32[8,1,768]{2,1,0:T(1,128)}), f32[8,1,768]{2,1,0:T(1,128)S(1)}, u32[]{:S(2)}, u32[]{:S(2)}) %all-to-all-start.5) | async-done | bytes 24608 | tf_op jit(solution)/shard_map/all_to_all | solution.py:37
  894.5 3.3 all-to-all-start.2
  897.9 0.0 copy-done.2
  897.9 0.7 multiply_reduce_fusion
  899.2 0.7 reduce_sum.84
  900.5 12.3 %all-to-all-done.2 = f32[8,1,768]{2,1,0:T(1,128)S(1)} async-done(((f32[8,1,768]{2,1,0:T(1,128)}), f32[8,1,768]{2,1,0:T(1,128)S(1)}, u32[]{:S(2)}, u32[]{:S(2)}) %all-to-all-start.2) | async-done | bytes 24608 | tf_op jit(solution)/shard_map/all_to_all | solution.py:37
  912.8 0.7 add_convert_fusion
Async XLA Ops:
  7.2 166.8 %copy-start = (bf16[768,384]{1,0:T(8,128)(2,1)S(1)}, bf16[768,384]{1,0:T(8,128)(2,1)}, u32[]{:S(2)}) copy-start(bf16[768,384]{1,0:T(8,128)(2,1)} %param.5) | copy-start | bytes 1769476
  7.2 418.1 %all-gather.7.cloned.1.call-start = ((), (), s32[]{:S(2)}) async-start(), calls=%async_computation.6 | async-start | bytes 7077888 | tf_op jit(solution)/shard_map/all_gather | solution.py:10
  174.0 1.5 copy-start.3
  175.4 502.8 %all-gather.9.cloned.1.call-start = ((), (), s32[]{:S(2)}) async-start(), calls=%async_computation.7 | async-start | bytes 7077888 | tf_op jit(solution)/shard_map/all_gather | solution.py:10
  385.3 38.5 %copy-start.1 = (bf16[384,768]{1,0:T(8,128)(2,1)S(1)}, bf16[384,768]{1,0:T(8,128)(2,1)}, u32[]{:S(2)}) copy-start(bf16[384,768]{1,0:T(8,128)(2,1)} %param.6) | copy-start | bytes 1769476
  686.6 102.4 %all-to-all-start.4 = ((f32[8,64,1,768]{3,0,2,1:T(8,128)}), f32[8,64,1,768]{3,0,2,1:T(8,128)}, u32[]{:S(2)}, u32[]{:S(2)}) async-start(f32[8,64,1,768]{3,0,2,1:T(8,128)} %copy.13), calls=%async_computation.4 | async-start | bytes 3145728 | tf_op jit(solution)/shard_map/all_to_all | solution.py:36
  789.0 82.1 %all-to-all-start.1 = ((f32[8,64,1,768]{3,0,2,1:T(8,128)}), f32[8,64,1,768]{3,0,2,1:T(8,128)}, u32[]{:S(2)}, u32[]{:S(2)}) async-start(f32[8,64,1,768]{3,0,2,1:T(8,128)} %copy.11), calls=%async_computation.1 | async-start | bytes 3145728 | tf_op jit(solution)/shard_map/all_to_all | solution.py:36
  871.1 23.4 %all-to-all-start.5 = ((f32[8,1,768]{2,1,0:T(1,128)}), f32[8,1,768]{2,1,0:T(1,128)S(1)}, u32[]{:S(2)}, u32[]{:S(2)}) async-start(f32[8,1,768]{2,1,0:T(1,128)} %reduce_sum.83), calls=%async_computation.5 | async-start | bytes 49152 | tf_op jit(solution)/shard_map/all_to_all | solution.py:37
  879.6 18.3 %copy-start.2 = (bf16[1,6144]{1,0:T(2,128)(2,1)S(1)}, bf16[1,6144]{1,0:T(2,128)(2,1)}, u32[]{:S(2)}) copy-start(bf16[1,6144]{1,0:T(2,128)(2,1)} %param.4) | copy-start | bytes 36868
  894.5 18.2 %all-to-all-start.2 = ((f32[8,1,768]{2,1,0:T(1,128)}), f32[8,1,768]{2,1,0:T(1,128)S(1)}, u32[]{:S(2)}, u32[]{:S(2)}) async-start(f32[8,1,768]{2,1,0:T(1,128)} %reduce_sum.80), calls=%async_computation.2 | async-start | bytes 49152 | tf_op jit(solution)/shard_map/all_to_all | solution.py:37
Sparse Core Ops, SparseCore 0:
  175.6 226.2 all-gather.6
  425.4 252.7 all-gather.8
